TPU v7x, 256 devices: a whole 4x4x8 slice. The times are simulated.
256 devices in a mesh: lat: 16 (over y_lo, x, core), lon: 16 (over z, y_hi).
Axes of the slice: x: 4, y: 4 (y_hi: 2, y_lo: 2; y = y_hi * 2 + y_lo), z: 8, core: 2. Of those that a mesh axis runs over, the one named last changes fastest.
Arguments:
- fields: bfloat16 [768, 2048, 128], P('lat', 'lon'), may hold values from -6 to 6
- wet_mask: int32 [768, 2048], P('lat', 'lon'), may hold values 0 or 1
- conv_kernel: float32 [2, 49, 128], replicated, may hold values from -0.875 to 0.875
- conv_bias: float32 [2, 128], replicated, may hold values from -3 to 3
- norm_gain: float32 [2, 128], replicated, may hold values from 0.5 to 1.5
- norm_bias: float32 [2, 128], replicated, may hold values from -2 to 2
- in_weight: bfloat16 [2, 128, 512], replicated, may hold values from -0.5 to 0.5
- in_bias: float32 [2, 512], replicated, may hold values from -3 to 3
- out_weight: bfloat16 [2, 512, 128], replicated, may hold values from -0.25 to 0.25
- out_bias: float32 [2, 128], replicated, may hold values from -2 to 2
- layer_scale: float32 [2, 128], replicated, may hold values from 0.5 to 1.5
Outputs:
- result: bfloat16 [768, 2048, 128], P('lat', 'lon')
Inputs may be any that keep to these rules, and one draw needn't show every extreme that they name: wet_mask holds only 0 and 1.
All inputs are finite; a program needn't handle non-finite values. No bound on the sum of `wet_mask` on one device may be relied on, other than what follows from the above.
Results may differ from a plain program's by a relative error of at most 0.0057.
Values may be sent and summed in bfloat16 or wider, within the bound.
A program may use at most 64 MiB of HBM per device.

v0:
```python
import jax, jax.numpy as jnp, functools
from jax import lax
from jax.experimental import pallas as pl
from jax.experimental.pallas import tpu as pltpu
from jax.sharding import PartitionSpec as P
BF=jnp.bfloat16; F=jnp.float32
R=4
def iota(s,d): return lax.broadcasted_iota(jnp.int32,s,d)
def dot(a,b): return jnp.dot(a,b,preferred_element_type=F)
def tree(v):
    while len(v)>1:
        v=[v[i]+v[i+1] if i+1<len(v) else v[i] for i in range(0,len(v),2)]
    return v[0]
def conv_row(XG, KF, bias, C, row, at):
    acc=[bias]*8
    for r in range(7):
        xs=[XG[row+r,k] for k in range(14)]
        ws=[]
        for s in range(7):
            w=KF[7*r+s]
            ws.append(jnp.concatenate([w,w],0).astype(BF))
        for k in range(8):
            acc[k]=acc[k]+tree([ws[s]*xs[k+s] for s in range(7)]).astype(F)
    for k in range(8):
        C[at*128+k*16:at*128+k*16+16,:]=acc[k]
def mlp_rows(C, XG, Y, row0, W1E, W2, VM, gain, nb, b2, ls):
    M=R*128
    c=C[...]
    cen=c-dot(c.astype(BF),VM)
    var=dot((cen*cen).astype(BF),VM)
    normed=(cen*lax.rsqrt(var+1e-6)*gain+nb).astype(BF)
    ones=jnp.where(iota((M,128),1)<3,1.0,0.0).astype(BF)
    t=dot(jnp.concatenate([normed,ones],1),W1E[...])
    g=(t*lax.erf(t*1.4142135623730951)+t).astype(BF)
    y=(dot(g,W2[...])+b2)*ls
    for rr in range(R):
        for k in range(8):
            res=XG[row0+rr+3,k+3].astype(F)
            Y[row0+rr,k]=(res+y[rr*128+k*16:rr*128+k*16+16]).astype(BF)
def kernel(idx, st, south, north, side, CK, cb, gain, nb, W1, b1, W2, b2, ls, out, XG, KF, W1E, W2S, C0, C1, Y):
    def src_matrix():
        n=iota((224,144),0); c=iota((224,144),1)
        col=8*(n%16)+n//16
        src=jnp.where(col<3,128+col,jnp.where(col>=131,col,col-3))
        return jnp.where(src==c,1.0,0.0).astype(BF)
    G=src_matrix()
    n=iota((128,128),0); c=iota((128,128),1)
    U=jnp.where((n%8)*16+n//8==c,1.0,0.0).astype(BF)
    VM=jnp.full((128,128),1/128,BF)
    for t in range(49):
        KF[t]=jnp.broadcast_to(CK[idx,t:t+1,:],(8,128))
    W1E[:128]=W1[idx]*BF(0.5)
    bb=b1[idx:idx+1]*0.5
    hi=bb.astype(BF).astype(F); lo=(bb-hi).astype(BF).astype(F); l2=bb-hi-lo
    z=iota((128,512),0)
    W1E[128:]=jnp.where(z==0,hi,jnp.where(z==1,lo,jnp.where(z==2,l2,0.0))).astype(BF)
    W2S=W2.at[idx]
    def put(i,mid,sd):
        XG[i]=dot(G,jnp.concatenate([mid,sd],0)).astype(BF).reshape(14,16,128)
    def prep(i,c):
        put(i+3,st[i],side[i+3]); return c
    lax.fori_loop(0,48,prep,0,unroll=2)
    for i in range(3):
        put(i,south[i],side[i]); put(51+i,north[i],side[51+i])
    bias=jnp.broadcast_to(cb[idx:idx+1],(16,128))
    def A(C,row0):
        for rr in range(R): conv_row(XG,KF,bias,C,row0+rr,rr)
    B=lambda Cx,row0: mlp_rows(Cx,XG,Y,row0,W1E,W2S,VM,gain[idx:idx+1],nb[idx:idx+1],b2[idx:idx+1],ls[idx:idx+1])
    n=48//R
    A(C0,0)
    def body(j,c):
        r0=j*2*R
        B(C0,r0); A(C1,r0+R)
        B(C1,r0+R); A(C0,r0+2*R)
        return c
    lax.fori_loop(0,n//2-1,body,0)
    r0=(n-2)*R
    B(C0,r0); A(C1,r0+R)
    B(C1,r0+R)
    def fin(i,c):
        out[i]=dot(U,Y[i].reshape(128,128)).astype(BF)
        return c
    lax.fori_loop(0,48,fin,0,unroll=2)
def block(idx, st, south, north, side, *w):
    vm=pl.BlockSpec(memory_space=pltpu.VMEM)
    return pl.pallas_call(functools.partial(kernel,idx),out_shape=jax.ShapeDtypeStruct((48,128,128),BF),
      in_specs=[vm]*13,out_specs=vm,
      scratch_shapes=[pltpu.VMEM((54,14,16,128),BF),pltpu.VMEM((49,8,128),F),pltpu.VMEM((256,512),BF),pltpu.VMEM((8,128),F),pltpu.VMEM((R*128,128),F),pltpu.VMEM((R*128,128),F),pltpu.VMEM((48,8,16,128),BF)],
      compiler_params=pltpu.CompilerParams(vmem_limit_bytes=60<<20),
      cost_estimate=pl.CostEstimate(flops=2*10**9,bytes_accessed=4*10**6,transcendentals=0),
      name=f"block{idx}",
    )(st,south,north,side,*w)

def halos(state):
    n = lax.axis_size("lon"); m = lax.axis_size("lat")
    up = [(i, (i + 1) % n) for i in range(n)]
    left = lax.ppermute(state[:, -3:], "lon", up)
    right = lax.ppermute(state[:, :3], "lon", [(j, i) for i, j in up])
    side = jnp.concatenate([left, right], 1)
    top = jnp.concatenate([state[-3:], side[-3:]], 1)
    bot = jnp.concatenate([state[:3], side[:3]], 1)
    south = lax.ppermute(top, "lat", [(i, i + 1) for i in range(m - 1)])
    ext = jnp.concatenate([top[:, 128:131], top[:, :128], top[:, 131:]], 1)[::-1, ::-1]
    fold = jnp.concatenate([ext[:, 3:131], ext[:, :3], ext[:, 131:]], 1)
    is_top = lax.axis_index("lat") == m - 1
    north = lax.ppermute(bot, "lat", [(i + 1, i) for i in range(m - 1)])
    route = [((m - 1) * n + l, (m - 1) * n + n - 1 - l) for l in range(n)]
    fold = lax.ppermute(fold, ("lat", "lon"), route)
    north = jnp.where(is_top, fold, north)
    full = jnp.concatenate([south[:, 128:], side, north[:, 128:]], 0)
    full = jnp.pad(full, ((0, 0), (0, 10), (0, 0)))
    return south[:, :128], north[:, :128], full
def shards(fields, wet_mask, *w):
    mask_bf = wet_mask.astype(BF)[:, :, None]
    state = fields * mask_bf
    for index in range(2):
        south, north, side = halos(state)
        state = block(index, state, south, north, side, *w)
    return state * mask_bf
def solution(mesh):
    return jax.shard_map(shards, mesh=mesh, in_specs=(P("lat", "lon", None), P("lat", "lon")) + (P(),) * 9,
        out_specs=P("lat", "lon", None), check_vma=False)
```

profile of v0, /device:TPU:63, one launch (start us, length us, event | category | flops | bytes accessed | tf_op | source)
XLA Modules:
  0.0 106.9 jit_solution(3783603123300461087)
XLA Ops:
  0.0 0.7 convert_element_type.6
  0.7 2.1 %broadcast_multiply_fusion.1.st = bf16[48,128,128]{2,1,0:T(8,128)(2,1)S(1)} fusion(bf16[48,128,128]{2,1,0:T(8,128)(2,1)} %param.11, bf16[48,128]{1,0:T(8,128)(2,1)S(1)} %convert_element_type.6), kind=kLoop, calls=%fused_computation.1 | loop fusion | flops 786432 | bytes 3158016 | tf_op jit(solution)/shard_map/mul | solution.py:115
  2.9 2.4 %collective-permute-start = (bf16[48,3,128]{2,1,0:T(4,128)(2,1)S(1)}, bf16[48,3,128]{2,1,0:T(4,128)(2,1)S(1)}, u32[]{:S(2)}, u32[]{:S(2)}) collective-permute-start(bf16[48,3,128]{2,1,0:T(4,128)(2,1)S(1)} %get-tuple-element.11), channel_id=1, source_target_pairs={{0,1},{1,2},{2,3},{3,4},{4,5},{5,6},{6,7},{7,8},{8,9},{9,10},{10,1... | collective-permute-start | bytes 110600 | tf_op jit(solution)/shard_map/ppermute | solution.py:97
  6.1 1.3 %collective-permute-done = bf16[48,3,128]{2,1,0:T(4,128)(2,1)S(1)} collective-permute-done((bf16[48,3,128]{2,1,0:T(4,128)(2,1)S(1)}, bf16[48,3,128]{2,1,0:T(4,128)(2,1)S(1)}, u32[]{:S(2)}, u32[]{:S(2)}) %collective-permute-start) | collective-permute-done | bytes 36896 | tf_op jit(solution)/shard_map/ppermute | solution.py:97
  7.5 3.2 %collective-permute-done.1 = bf16[48,3,128]{2,1,0:T(4,128)(2,1)S(1)} collective-permute-done((bf16[48,3,128]{2,1,0:T(4,128)(2,1)S(1)}, bf16[48,3,128]{2,1,0:T(4,128)(2,1)S(1)}, u32[]{:S(2)}, u32[]{:S(2)}) %collective-permute-start.1) | collective-permute-done | bytes 36896 | tf_op jit(solution)/shard_map/ppermute | solution.py:98
  10.7 4.0 %collective-permute-start.4 = (bf16[3,134,128]{2,1,0:T(8,128)(2,1)S(1)}, bf16[3,134,128]{2,1,0:T(8,128)(2,1)S(1)}, u32[]{:S(2)}, u32[]{:S(2)}) collective-permute-start(bf16[3,134,128]{2,1,0:T(8,128)(2,1)S(1)} %get-tuple-element.15), channel_id=1, source_target_pairs={{16,0},{32,16},{48,32},{64,48},{80,64},{96,80},{112,96},{128,112},... | collective-permute-start | bytes 308744 | tf_op jit(solution)/shard_map/ppermute | solution.py:106
  14.8 7.0 %collective-permute-start.3 = (bf16[3,134,128]{2,1,0:T(8,128)(2,1)S(1)}, bf16[3,134,128]{2,1,0:T(8,128)(2,1)S(1)}, u32[]{:S(2)}, u32[]{:S(2)}) collective-permute-start(bf16[3,134,128]{2,1,0:T(8,128)(2,1)S(1)} %pad_maximum_fusion.4), channel_id=1, source_target_pairs={{240,255},{241,254},{242,253},{243,252},{244,251},{245,250},{246,2... | collective-permute-start | bytes 308744 | tf_op jit(solution)/shard_map/ppermute | solution.py:108
  22.4 1.3 %collective-permute-start.2 = (bf16[3,134,128]{2,1,0:T(8,128)(2,1)S(1)}, bf16[3,134,128]{2,1,0:T(8,128)(2,1)S(1)}, u32[]{:S(2)}, u32[]{:S(2)}) collective-permute-start(bf16[3,134,128]{2,1,0:T(8,128)(2,1)S(1)} %get-tuple-element.16), channel_id=1, source_target_pairs={{0,16},{16,32},{32,48},{48,64},{64,80},{80,96},{96,112},{112,128},... | collective-permute-start | bytes 308744 | tf_op jit(solution)/shard_map/ppermute | solution.py:102
  23.7 1.9 %collective-permute-done.3 = bf16[3,134,128]{2,1,0:T(8,128)(2,1)S(1)} collective-permute-done((bf16[3,134,128]{2,1,0:T(8,128)(2,1)S(1)}, bf16[3,134,128]{2,1,0:T(8,128)(2,1)S(1)}, u32[]{:S(2)}, u32[]{:S(2)}) %collective-permute-start.3) | collective-permute-done | bytes 102944 | tf_op jit(solution)/shard_map/ppermute | solution.py:108
  26.9 0.8 fusion.9.side
  27.7 25.6 %block0.1.st = bf16[48,128,128]{2,1,0:T(8,128)(2,1)} custom-call(bf16[48,128,128]{2,1,0:T(8,128)(2,1)} %copy-done, bf16[3,128,128]{2,1,0:T(8,128)(2,1)} %slice.137.south, bf16[3,128,128]{2,1,0:T(8,128)(2,1)} %slice.141.north, bf16[54,16,128]{2,1,0:T(8,128)(2,1)} %fusion.9.side, f32[2,49,128]{2,1,0:T(8,128)} %copy.12.CK, f32[2,128]{1,0:T(2,128)} %cb.3, ...), custom_call_target="tpu_custom_call" | custom-call | flops 2000000000 | bytes 4000000 | tf_op jit(solution)/shard_map/block0/pallas_call | solution.py:86
  53.3 1.0 fusion.19
  54.3 2.1 %collective-permute-start.5 = (bf16[48,3,128]{2,1,0:T(4,128)(2,1)S(1)}, bf16[48,3,128]{2,1,0:T(4,128)(2,1)S(1)}, u32[]{:S(2)}, u32[]{:S(2)}) collective-permute-start(bf16[48,3,128]{2,1,0:T(4,128)(2,1)S(1)} %get-tuple-element.7), channel_id=1, source_target_pairs={{0,1},{1,2},{2,3},{3,4},{4,5},{5,6},{6,7},{7,8},{8,9},{9,10},{10,1... | collective-permute-start | bytes 110600 | tf_op jit(solution)/shard_map/ppermute | solution.py:97
  56.4 0.9 collective-permute-start.6
  57.4 1.0 fusion.18
  58.5 1.0 collective-permute-done.5
  59.5 2.3 %collective-permute-done.6 = bf16[48,3,128]{2,1,0:T(4,128)(2,1)S(1)} collective-permute-done((bf16[48,3,128]{2,1,0:T(4,128)(2,1)S(1)}, bf16[48,3,128]{2,1,0:T(4,128)(2,1)S(1)}, u32[]{:S(2)}, u32[]{:S(2)}) %collective-permute-start.6) | collective-permute-done | bytes 36896 | tf_op jit(solution)/shard_map/ppermute | solution.py:98
  61.8 3.5 %collective-permute-start.9 = (bf16[3,134,128]{2,1,0:T(8,128)(2,1)S(1)}, bf16[3,134,128]{2,1,0:T(8,128)(2,1)S(1)}, u32[]{:S(2)}, u32[]{:S(2)}) collective-permute-start(bf16[3,134,128]{2,1,0:T(8,128)(2,1)S(1)} %get-tuple-element.13), channel_id=1, source_target_pairs={{16,0},{32,16},{48,32},{64,48},{80,64},{96,80},{112,96},{128,112},... | collective-permute-start | bytes 308744 | tf_op jit(solution)/shard_map/ppermute | solution.py:106
  65.4 4.2 %collective-permute-start.8 = (bf16[3,134,128]{2,1,0:T(8,128)(2,1)S(1)}, bf16[3,134,128]{2,1,0:T(8,128)(2,1)S(1)}, u32[]{:S(2)}, u32[]{:S(2)}) collective-permute-start(bf16[3,134,128]{2,1,0:T(8,128)(2,1)S(1)} %pad_maximum_fusion.5), channel_id=1, source_target_pairs={{240,255},{241,254},{242,253},{243,252},{244,251},{245,250},{246,2... | collective-permute-start | bytes 308744 | tf_op jit(solution)/shard_map/ppermute | solution.py:108
  69.5 1.5 %collective-permute-start.7 = (bf16[3,134,128]{2,1,0:T(8,128)(2,1)S(1)}, bf16[3,134,128]{2,1,0:T(8,128)(2,1)S(1)}, u32[]{:S(2)}, u32[]{:S(2)}) collective-permute-start(bf16[3,134,128]{2,1,0:T(8,128)(2,1)S(1)} %get-tuple-element.14), channel_id=1, source_target_pairs={{0,16},{16,32},{32,48},{48,64},{64,80},{80,96},{96,112},{112,128},... | collective-permute-start | bytes 308744 | tf_op jit(solution)/shard_map/ppermute | solution.py:102
  71.0 5.2 %collective-permute-done.8 = bf16[3,134,128]{2,1,0:T(8,128)(2,1)S(1)} collective-permute-done((bf16[3,134,128]{2,1,0:T(8,128)(2,1)S(1)}, bf16[3,134,128]{2,1,0:T(8,128)(2,1)S(1)}, u32[]{:S(2)}, u32[]{:S(2)}) %collective-permute-start.8) | collective-permute-done | bytes 102944 | tf_op jit(solution)/shard_map/ppermute | solution.py:108
  77.5 0.8 fusion.12.side
  78.3 25.6 %block1.1 = bf16[48,128,128]{2,1,0:T(8,128)(2,1)} custom-call(bf16[48,128,128]{2,1,0:T(8,128)(2,1)} %block0.1.st, bf16[3,128,128]{2,1,0:T(8,128)(2,1)} %slice.147.south, bf16[3,128,128]{2,1,0:T(8,128)(2,1)} %slice.151.north, bf16[54,16,128]{2,1,0:T(8,128)(2,1)} %fusion.12.side, f32[2,49,128]{2,1,0:T(8,128)} %copy.12.CK, f32[2,128]{1,0:T(2,128)} %cb.3, ...), custom_call_target="tpu_custom_call" | custom-call | flops 2000000000 | bytes 4000000 | tf_op jit(solution)/shard_map/block1/pallas_call | solution.py:86
  103.9 3.0 %broadcast_multiply_fusion = bf16[48,128,128]{2,1,0:T(8,128)(2,1)} fusion(bf16[48,128,128]{2,1,0:T(8,128)(2,1)} %block1.1, bf16[48,128]{1,0:T(8,128)(2,1)S(1)} %convert_element_type.6), kind=kLoop, calls=%fused_computation | loop fusion | flops 786432 | bytes 3158016 | tf_op jit(solution)/shard_map/mul | solution.py:119
  (36 shorter events, 4.5 us)
Async XLA Ops:
  0.7 21.0 %copy-start.1 = (f32[2,49,128]{2,0,1:T(2,128)S(1)}, f32[2,49,128]{2,0,1:T(2,128)}, u32[]{:S(2)}) copy-start(f32[2,49,128]{2,0,1:T(2,128)} %param.13) | copy-start | bytes 150532
  2.9 24.9 %copy-start = (bf16[48,128,128]{2,1,0:T(8,128)(2,1)}, bf16[48,128,128]{2,1,0:T(8,128)(2,1)S(1)}, u32[]{:S(2)}) copy-start(bf16[48,128,128]{2,1,0:T(8,128)(2,1)S(1)} %broadcast_multiply_fusion.1.st) | copy-start | bytes 4718596
  2.9 4.5 %collective-permute-start = (bf16[48,3,128]{2,1,0:T(4,128)(2,1)S(1)}, bf16[48,3,128]{2,1,0:T(4,128)(2,1)S(1)}, u32[]{:S(2)}, u32[]{:S(2)}) collective-permute-start(bf16[48,3,128]{2,1,0:T(4,128)(2,1)S(1)} %get-tuple-element.11), channel_id=1, source_target_pairs={{0,1},{1,2},{2,3},{3,4},{4,5},{5,6},{6,7},{7,8},{8,9},{9,10},{10,1... | collective-permute-start | bytes 110600 | tf_op jit(solution)/shard_map/ppermute | solution.py:97
  5.3 5.3 %collective-permute-start.1 = (bf16[48,3,128]{2,1,0:T(4,128)(2,1)S(1)}, bf16[48,3,128]{2,1,0:T(4,128)(2,1)S(1)}, u32[]{:S(2)}, u32[]{:S(2)}) collective-permute-start(bf16[48,3,128]{2,1,0:T(4,128)(2,1)S(1)} %get-tuple-element.12), channel_id=1, source_target_pairs={{1,0},{2,1},{3,2},{4,3},{5,4},{6,5},{7,6},{8,7},{9,8},{10,9},{11,1... | collective-permute-start | bytes 110600 | tf_op jit(solution)/shard_map/ppermute | solution.py:98
  10.7 12.9 %collective-permute-start.4 = (bf16[3,134,128]{2,1,0:T(8,128)(2,1)S(1)}, bf16[3,134,128]{2,1,0:T(8,128)(2,1)S(1)}, u32[]{:S(2)}, u32[]{:S(2)}) collective-permute-start(bf16[3,134,128]{2,1,0:T(8,128)(2,1)S(1)} %get-tuple-element.15), channel_id=1, source_target_pairs={{16,0},{32,16},{48,32},{64,48},{80,64},{96,80},{112,96},{128,112},... | collective-permute-start | bytes 308744 | tf_op jit(solution)/shard_map/ppermute | solution.py:106
  14.8 10.8 %collective-permute-start.3 = (bf16[3,134,128]{2,1,0:T(8,128)(2,1)S(1)}, bf16[3,134,128]{2,1,0:T(8,128)(2,1)S(1)}, u32[]{:S(2)}, u32[]{:S(2)}) collective-permute-start(bf16[3,134,128]{2,1,0:T(8,128)(2,1)S(1)} %pad_maximum_fusion.4), channel_id=1, source_target_pairs={{240,255},{241,254},{242,253},{243,252},{244,251},{245,250},{246,2... | collective-permute-start | bytes 308744 | tf_op jit(solution)/shard_map/ppermute | solution.py:108
  22.4 3.9 %collective-permute-start.2 = (bf16[3,134,128]{2,1,0:T(8,128)(2,1)S(1)}, bf16[3,134,128]{2,1,0:T(8,128)(2,1)S(1)}, u32[]{:S(2)}, u32[]{:S(2)}) collective-permute-start(bf16[3,134,128]{2,1,0:T(8,128)(2,1)S(1)} %get-tuple-element.16), channel_id=1, source_target_pairs={{0,16},{16,32},{32,48},{48,64},{64,80},{80,96},{96,112},{112,128},... | collective-permute-start | bytes 308744 | tf_op jit(solution)/shard_map/ppermute | solution.py:102
  54.3 5.1 %collective-permute-start.5 = (bf16[48,3,128]{2,1,0:T(4,128)(2,1)S(1)}, bf16[48,3,128]{2,1,0:T(4,128)(2,1)S(1)}, u32[]{:S(2)}, u32[]{:S(2)}) collective-permute-start(bf16[48,3,128]{2,1,0:T(4,128)(2,1)S(1)} %get-tuple-element.7), channel_id=1, source_target_pairs={{0,1},{1,2},{2,3},{3,4},{4,5},{5,6},{6,7},{7,8},{8,9},{9,10},{10,1... | collective-permute-start | bytes 110600 | tf_op jit(solution)/shard_map/ppermute | solution.py:97
  56.4 5.3 %collective-permute-start.6 = (bf16[48,3,128]{2,1,0:T(4,128)(2,1)S(1)}, bf16[48,3,128]{2,1,0:T(4,128)(2,1)S(1)}, u32[]{:S(2)}, u32[]{:S(2)}) collective-permute-start(bf16[48,3,128]{2,1,0:T(4,128)(2,1)S(1)} %get-tuple-element.8), channel_id=1, source_target_pairs={{1,0},{2,1},{3,2},{4,3},{5,4},{6,5},{7,6},{8,7},{9,8},{10,9},{11,1... | collective-permute-start | bytes 110600 | tf_op jit(solution)/shard_map/ppermute | solution.py:98
  61.8 9.2 %collective-permute-start.9 = (bf16[3,134,128]{2,1,0:T(8,128)(2,1)S(1)}, bf16[3,134,128]{2,1,0:T(8,128)(2,1)S(1)}, u32[]{:S(2)}, u32[]{:S(2)}) collective-permute-start(bf16[3,134,128]{2,1,0:T(8,128)(2,1)S(1)} %get-tuple-element.13), channel_id=1, source_target_pairs={{16,0},{32,16},{48,32},{64,48},{80,64},{96,80},{112,96},{128,112},... | collective-permute-start | bytes 308744 | tf_op jit(solution)/shard_map/ppermute | solution.py:106
  65.4 10.8 %collective-permute-start.8 = (bf16[3,134,128]{2,1,0:T(8,128)(2,1)S(1)}, bf16[3,134,128]{2,1,0:T(8,128)(2,1)S(1)}, u32[]{:S(2)}, u32[]{:S(2)}) collective-permute-start(bf16[3,134,128]{2,1,0:T(8,128)(2,1)S(1)} %pad_maximum_fusion.5), channel_id=1, source_target_pairs={{240,255},{241,254},{242,253},{243,252},{244,251},{245,250},{246,2... | collective-permute-start | bytes 308744 | tf_op jit(solution)/shard_map/ppermute | solution.py:108
  69.5 7.4 %collective-permute-start.7 = (bf16[3,134,128]{2,1,0:T(8,128)(2,1)S(1)}, bf16[3,134,128]{2,1,0:T(8,128)(2,1)S(1)}, u32[]{:S(2)}, u32[]{:S(2)}) collective-permute-start(bf16[3,134,128]{2,1,0:T(8,128)(2,1)S(1)} %get-tuple-element.14), channel_id=1, source_target_pairs={{0,16},{16,32},{32,48},{48,64},{64,80},{80,96},{96,112},{112,128},... | collective-permute-start | bytes 308744 | tf_op jit(solution)/shard_map/ppermute | solution.py:102
where the time goes:
time: 107 us
  Pallas kernels  51.2 us (48%)
  starting transfers between devices  27.5 us (26%)
  waiting for transfers between devices  14.9 us (14%)
  other arithmetic  7.54 us (7%)
  local copies, waits for them, and re-layouts  5.61 us (5%)
    pallas_call x2, Pallas kernels, block(): pl.pallas_call(functools.partial(kernel, idx), out_shape=jax.ShapeDtypeSt...  51.2 us
    ppermute x2, starting transfers between devices, halos(): fold = lax.ppermute(fold, ('lat', 'lon'), route)  11.1 us
    ppermute x2, starting transfers between devices, halos(): north = lax.ppermute(bot, 'lat', [(i + 1, i) for i in range(m - 1)])  7.51 us
    ppermute x2, waiting for transfers between devices, halos(): fold = lax.ppermute(fold, ('lat', 'lon'), route)  7.12 us
    ppermute x2, waiting for transfers between devices, halos(): right = lax.ppermute(state[:, :3], 'lon', [(j, i) for i, j in up])  5.44 us
    ppermute x2, starting transfers between devices, halos(): left = lax.ppermute(state[:, -3:], 'lon', up)  4.5 us
    mul x1, other arithmetic, shards(): return state * mask_bf  2.98 us
    ppermute x2, starting transfers between devices, halos(): south = lax.ppermute(top, 'lat', [(i, i + 1) for i in range(m - 1)])  2.75 us
  transfers between devices with their start and end apart: 10, of which 6 were waited for; matrix products, arithmetic and copies ran while one was open for 3% of the time, Pallas kernels for 0%

commit v1 on v0

v1 whole, which is shorter than its diff:
```python
import functools

import jax
import jax.numpy as jnp
from jax import lax
from jax.experimental import pallas as pl
from jax.experimental.pallas import tpu as pltpu
from jax.sharding import PartitionSpec as P

BF, F = jnp.bfloat16, jnp.float32
R = 4
ROWS, COLS, C = 48, 128, 128
N = ROWS // R
MESH = pl.DeviceIdType.MESH


def iota(shape, d):
    return lax.broadcasted_iota(jnp.int32, shape, d)


def onehot(cond):
    return jnp.where(cond, 1.0, 0.0).astype(BF)


def dot(a, b):
    return jnp.dot(a, b, preferred_element_type=F)


def tree(v):
    while len(v) > 1:
        v = [v[i] + v[i + 1] if i + 1 < len(v) else v[i] for i in range(0, len(v), 2)]
    return v[0]


def chunk0(s):
    return jnp.where(s < 8, s + 1, jnp.where(s == 8, 0, jnp.where(s == 9, 11, s - 1)))


def chunk1(s):
    return jnp.where(s < 7, s + 2, jnp.where(s == 7, 1, jnp.where(s < 10, s + 1, (s - 10) * 11)))


def conv(XG, KF, bias, acc_ref, row0):
    for rr in range(R):
        acc = [bias] * 8
        for r in range(7):
            xs = [XG[row0 + rr + r, k] for k in range(14)]
            ws = []
            for s in range(7):
                w = KF[7 * r + s]
                ws.append(jnp.concatenate([w, w], 0).astype(BF))
            for k in range(8):
                acc[k] = acc[k] + tree([ws[s] * xs[k + s] for s in range(7)]).astype(F)
        for k in range(8):
            acc_ref[rr * 128 + k * 16 : rr * 128 + k * 16 + 16, :] = acc[k]


def mlp(acc_ref, VM, W1E, W2, gain, nb, b2, ls):
    c = acc_ref[...]
    cen = c - dot(c.astype(BF), VM)
    var = dot((cen * cen).astype(BF), VM)
    normed = (cen * lax.rsqrt(var + 1e-6) * gain + nb).astype(BF)
    ones = onehot(iota((R * 128, 128), 1) < 3)
    t = dot(jnp.concatenate([normed, ones], 1), W1E[...])
    g = (t * lax.erf(t * 1.4142135623730951) + t).astype(BF)
    return (dot(g, W2[...]) + b2) * ls


def kernel(
    fields, mask, CK, cb, gain, nb, W1, b1, W2, b2, ls, out,
    NAT, XG0, XG1, CKV, KF, W1V, W1E, W2V, G4, H4, INS, UM, MG,
    acc0, acc1, EL, ER, LH, RH, FB, load_sem, send_sem, recv_sem, out_sem,
):
    lat, lon = lax.axis_index("lat"), lax.axis_index("lon")
    nlat, nlon = lax.axis_size("lat"), lax.axis_size("lon")
    right, left = lax.rem(lon + 1, nlon), lax.rem(lon + nlon - 1, nlon)
    fold = nlon - 1 - lon
    is_top, is_low = lat == nlat - 1, lat == 0
    not_top, not_low = lat < nlat - 1, lat > 0

    loads = [pltpu.make_async_copy(fields.at[pl.ds(12 * q, 12)], NAT.at[pl.ds(12 * q, 12)], load_sem.at[q]) for q in range(4)]
    loads += [
        pltpu.make_async_copy(CK, CKV, load_sem.at[4]),
        pltpu.make_async_copy(W1, W1V, load_sem.at[5]),
        pltpu.make_async_copy(W2, W2V, load_sem.at[6]),
    ]
    for cp in loads:
        cp.start()

    barrier = pltpu.get_barrier_semaphore()

    def greet(a, o):
        pl.semaphore_signal(barrier, inc=1, device_id={"lat": a, "lon": o}, device_id_type=MESH)

    greet(lat, left)
    greet(lat, right)

    @pl.when(not_low)
    def _():
        greet(lat - 1, lon)

    @pl.when(not_top)
    def _():
        greet(lat + 1, lon)

    @pl.when(is_top)
    def _():
        greet(lat, fold)

    def remote(src, dst, i, j, a, o):
        return pltpu.make_async_remote_copy(
            src_ref=src, dst_ref=dst, send_sem=send_sem.at[i], recv_sem=recv_sem.at[j],
            device_id={"lat": a, "lon": o}, device_id_type=MESH,
        )

    n, c = iota((256, 128), 0), iota((256, 128), 1)
    col = 8 * (n % 16) + n // 16 - 3
    h, hc = iota((128, 128), 0), iota((128, 128), 1)
    kk = h // 16
    g16 = h % 16
    ksrc = jnp.where(kk < 3, kk + 5, kk - 3)
    gsrc = jnp.where(kk < 3, g16 - 1, g16 + 1)
    hsrc = jnp.where((gsrc >= 0) & (gsrc < 16), ksrc * 16 + gsrc, -1)
    for rr in range(R):
        e = g16 - 4 * rr
        ok = (e >= 0) & (e < 3)
        en = n % 16 - 4 * rr
        okn = (en >= 0) & (en < 3)
        lsrc, rsrc = jnp.where(okn, en, -1), jnp.where(okn, 125 + en, -1)
        G4[rr] = onehot(jnp.where(n < 224, col, jnp.where(n < 240, lsrc, rsrc)) == c)
        hl, hr = jnp.where(ok, e * 16, -1), jnp.where(ok, (5 + e) * 16 + 15, -1)
        H4[rr] = onehot(jnp.where(kk < 6, hsrc, jnp.where(kk < 7, hl, hr)) == hc)
    m, mc = iota((96 * R, 32), 0), iota((96 * R, 32), 1)
    mr, mk, mg = m // 96, (m % 96) // 16, m % 16
    INS[...] = onehot(jnp.where(mk < 3, jnp.where(mg == 0, 4 * mr + mk, -1), jnp.where(mg == 15, 13 + 4 * mr + mk, -1)) == mc)
    UM[...] = onehot((h % 8) * 16 + h // 8 == hc)
    MG[...] = dot(mask[...].astype(F).astype(BF), onehot((hc % 16) * 8 + hc // 16 == h))
    VM = jnp.full((128, 128), 1 / 128, BF)

    def pairs(b, lo, hi, base):
        a, z = 16 * lo, 16 * (hi - lo)
        return (
            remote(ER.at[b, pl.ds(a, z)], LH.at[b, pl.ds(a, z)], base, base, lat, right),
            remote(EL.at[b, pl.ds(a, z)], RH.at[b, pl.ds(a, z)], base + 1, base + 1, lat, left),
        )

    cols0 = pairs(0, 0, 12, 0)
    colsA = pairs(1, 1, 9, 2)
    colsB = pairs(1, 0, 1, 4)
    colsC = pairs(1, 11, 12, 6)
    colsD = pairs(1, 9, 11, 8)
    cols1 = colsA + colsB + colsC + colsD

    def rows(XG, b):
        i = 10 + 3 * b
        north = remote(XG.at[pl.ds(48, 3)], XG.at[pl.ds(0, 3)], i, i, lat + 1, lon)
        across = remote(XG.at[pl.ds(48, 3)], FB.at[b], i + 1, i + 1, lat, fold)
        south = remote(XG.at[pl.ds(3, 3)], XG.at[pl.ds(51, 3)], i + 2, i + 2, lat - 1, lon)
        return north, across, south

    rows0, rows1 = rows(XG0, 0), rows(XG1, 1)

    def send_rows(copies):
        north, across, south = copies
        pl.when(not_top)(north.start)
        pl.when(is_top)(across.start)
        pl.when(not_low)(south.start)

    def wait_rows(XG, b, copies):
        north, across, south = copies
        pl.when(not_low)(north.wait_recv)

        @pl.when(is_low)
        def _():
            XG[0:3] = jnp.zeros((3, 14, 16, 128), BF)

        pl.when(not_top)(south.wait_recv)

        @pl.when(is_top)
        def _():
            across.wait_recv()
            flip = onehot(iota((224, 224), 0) + iota((224, 224), 1) == 223)
            for j in range(3):
                XG[51 + j] = dot(flip, FB[b, 2 - j].reshape(224, 128)).astype(BF).reshape(14, 16, 128)

    def insert(XG, b, ch):
        at = pl.ds(pl.multiple_of(16 * ch, 16), 16)
        o = dot(INS[...], jnp.concatenate([LH[b, at], RH[b, at]], 0)).astype(BF)
        for rr in range(R):
            row = R * ch + rr + 3
            XG[row, 0:3] = XG[row, 0:3] + o[rr * 96 : rr * 96 + 48].reshape(3, 16, 128)
            XG[row, 11:14] = XG[row, 11:14] + o[rr * 96 + 48 : rr * 96 + 96].reshape(3, 16, 128)

    def edges(b, ch, el, er):
        at = pl.ds(pl.multiple_of(16 * ch, 16), 16)
        EL[b, at] = el.astype(BF)
        ER[b, at] = er.astype(BF)

    def prep(ch, carry):
        el = er = None
        for rr in range(R):
            row = R * ch + rr
            mrow = jnp.broadcast_to(mask[pl.ds(row, 1), :].astype(F), (16, 128)).astype(BF)
            lhs = (G4[rr].reshape(16, 16, 128) * mrow[None]).reshape(256, 128)
            o = dot(lhs, NAT[row])
            XG0[row + 3] = o[:224].astype(BF).reshape(14, 16, 128)
            el = o[224:240] if el is None else el + o[224:240]
            er = o[240:256] if er is None else er + o[240:256]
        edges(0, ch, el, er)
        return carry

    for q in range(4):
        loads[q].wait()
        lax.fori_loop(3 * q, 3 * q + 3, prep, 0)

    @pl.when(not_low & not_top)
    def _():
        pl.semaphore_wait(barrier, 4)

    @pl.when(is_low)
    def _():
        pl.semaphore_wait(barrier, 3)

    @pl.when(is_top)
    def _():
        pl.semaphore_wait(barrier, 4)

    for cp in cols0:
        cp.start()
    for cp in loads[4:]:
        cp.wait()
    for b in range(2):
        for t in range(49):
            KF[b, t] = jnp.broadcast_to(CKV[b, t : t + 1, :], (8, 128))
        W1E[b, :128] = W1V[b] * BF(0.5)
        bb = b1[b : b + 1] * 0.5
        hi = bb.astype(BF).astype(F)
        lo = (bb - hi).astype(BF).astype(F)
        z = iota((128, 512), 0)
        W1E[b, 128:] = jnp.where(z == 0, hi, jnp.where(z == 1, lo, jnp.where(z == 2, bb - hi - lo, 0.0))).astype(BF)
    for cp in cols0:
        cp.wait_recv()

    def ins0(ch, carry):
        insert(XG0, 0, ch)
        return carry

    lax.fori_loop(0, N, ins0, 0)
    send_rows(rows0)

    def stage(b, XG):
        bias = jnp.broadcast_to(cb[b : b + 1], (16, 128))
        vec = [v[b : b + 1] for v in (gain, nb, b2, ls)]
        A = lambda acc, ch: conv(XG, KF.at[b], bias, acc, R * ch)

        def B(acc, ch):
            y = mlp(acc, VM, W1E.at[b], W2V.at[b], *vec)
            el = er = None
            for rr in range(R):
                row = R * ch + rr
                res = XG[row + 3, 3:11].reshape(128, 128).astype(F)
                x = (res + y[rr * 128 : rr * 128 + 128]).astype(BF)
                if b == 0:
                    XG1[row + 3, 3:11] = x.reshape(8, 16, 128)
                    o = dot(H4[rr], x)
                    XG1[row + 3, 0:3] = o[:48].astype(BF).reshape(3, 16, 128)
                    XG1[row + 3, 11:14] = o[48:96].astype(BF).reshape(3, 16, 128)
                    el = o[96:112] if el is None else el + o[96:112]
                    er = o[112:128] if er is None else er + o[112:128]
                else:
                    mrow = jnp.broadcast_to(MG[pl.ds(row, 1), :], (16, 128)).astype(BF)
                    lhs = (UM[...].reshape(8, 16, 128) * mrow[None]).reshape(128, 128)
                    NAT[row] = dot(lhs, x).astype(BF)
            if b == 0:
                edges(1, ch, el, er)

        return A, B

    A, B = stage(0, XG0)
    A(acc0, chunk0(0))

    def body0(j, carry):
        @pl.when(j == 3)
        def _():
            wait_rows(XG0, 0, rows0)

        B(acc0, chunk0(2 * j))
        A(acc1, chunk0(2 * j + 1))
        B(acc1, chunk0(2 * j + 1))
        A(acc0, chunk0(2 * j + 2))

        @pl.when(j == 3)
        def _():
            for cp in colsA:
                cp.start()

        @pl.when(j == 4)
        def _():
            for cp in colsB + colsC:
                cp.start()

        return carry

    lax.fori_loop(0, N // 2 - 1, body0, 0)
    B(acc0, chunk0(N - 2))
    A(acc1, chunk0(N - 1))
    B(acc1, chunk0(N - 1))
    for cp in colsD:
        cp.start()

    for cp in colsA:
        cp.wait_recv()

    def ins1(ch, carry):
        insert(XG1, 1, ch)
        return carry

    lax.fori_loop(1, 9, ins1, 0)
    A, B = stage(1, XG1)
    A(acc0, chunk1(0))

    def finish(ch):
        return pltpu.make_async_copy(NAT.at[pl.ds(R * ch, R)], out.at[pl.ds(R * ch, R)], out_sem.at[ch])

    def body1(j, carry):
        @pl.when(j == 1)
        def _():
            for cp in colsB + colsC + colsD:
                cp.wait_recv()
            insert(XG1, 1, 0)
            insert(XG1, 1, 11)
            insert(XG1, 1, 9)
            insert(XG1, 1, 10)
            send_rows(rows1)

        @pl.when(j == 4)
        def _():
            wait_rows(XG1, 1, rows1)

        B(acc0, chunk1(2 * j))
        A(acc1, chunk1(2 * j + 1))
        B(acc1, chunk1(2 * j + 1))
        A(acc0, chunk1(2 * j + 2))
        finish(chunk1(2 * j)).start()
        finish(chunk1(2 * j + 1)).start()
        return carry

    lax.fori_loop(0, N // 2 - 1, body1, 0)
    B(acc0, chunk1(N - 2))
    A(acc1, chunk1(N - 1))
    B(acc1, chunk1(N - 1))
    finish(chunk1(N - 2)).start()
    finish(chunk1(N - 1)).start()

    for cp in cols0 + cols1:
        cp.wait_send()
    for north, across, south in (rows0, rows1):
        pl.when(not_top)(north.wait_send)
        pl.when(is_top)(across.wait_send)
        pl.when(not_low)(south.wait_send)
    for ch in range(N):
        finish(ch).wait()


def shards(fields, wet_mask, *w):
    CK, cb, gain, nb, W1, b1, W2, b2, ls = w
    vm, hbm = pl.BlockSpec(memory_space=pltpu.VMEM), pl.BlockSpec(memory_space=pl.ANY)
    V = pltpu.VMEM
    return pl.pallas_call(
        kernel,
        out_shape=jax.ShapeDtypeStruct((ROWS, COLS, C), BF),
        in_specs=[hbm, vm, hbm, vm, vm, vm, hbm, vm, hbm, vm, vm],
        out_specs=hbm,
        scratch_shapes=[
            V((ROWS, COLS, C), BF), V((54, 14, 16, C), BF), V((54, 14, 16, C), BF),
            V((2, 49, C), F), V((2, 49, 8, C), F), V((2, 128, 512), BF), V((2, 256, 512), BF), V((2, 512, 128), BF),
            V((R, 256, 128), BF), V((R, 128, 128), BF), V((96 * R, 32), BF), V((128, 128), BF), V((ROWS, 128), F),
            V((R * 128, C), F), V((R * 128, C), F),
            V((2, 192, C), BF), V((2, 192, C), BF), V((2, 192, C), BF), V((2, 192, C), BF), V((2, 3, 14, 16, C), BF),
            pltpu.SemaphoreType.DMA((7,)), pltpu.SemaphoreType.DMA((16,)), pltpu.SemaphoreType.DMA((16,)), pltpu.SemaphoreType.DMA((N,)),
        ],
        compiler_params=pltpu.CompilerParams(vmem_limit_bytes=60 << 20, collective_id=0, has_side_effects=True),
        name="forecast",
    )(fields, wet_mask, *w)


def solution(mesh):
    return jax.shard_map(
        shards, mesh=mesh, in_specs=(P("lat", "lon", None), P("lat", "lon")) + (P(),) * 9,
        out_specs=P("lat", "lon", None), check_vma=False,
    )
```

time: 107 us -> 56.1 us (0.52)
  the two profiles are of different devices: /device:TPU:63 before, /device:TPU:4 now
where the time goes in v1:
time: 56.1 us; the launch traced here: 55.9 us
  Pallas kernels  51.7 us (92%)
  local copies, waits for them, and re-layouts  4.16 us (7%)
    pallas_call x1, Pallas kernels, shards(): pl.pallas_call(kernel, out_shape=jax.ShapeDtypeStruct((ROWS, COLS, C), BF...  51.7 us
    unnamed x2, local copies, waits for them, and re-layouts  4.16 us

profile of v1, /device:TPU:4, one launch (start us, length us, event | category | flops | bytes accessed | tf_op | source)
XLA Modules:
  0.0 55.9 jit_solution(17225393671466173889)
XLA Ops:
  0.0 1.4 %copy.12.CK = f32[2,49,128]{2,1,0:T(8,128)} copy(f32[2,49,128]{2,0,1:T(2,128)} %param.13) | data formatting | bytes 100352 | tf_op args[2]
  1.4 51.7 %forecast.1 = bf16[48,128,128]{2,1,0:T(8,128)(2,1)} custom-call(bf16[48,128,128]{2,1,0:T(8,128)(2,1)} %fields.1, s32[48,128]{1,0:T(8,128)} %mask.1, f32[2,49,128]{2,1,0:T(8,128)} %copy.12.CK, f32[2,128]{1,0:T(2,128)} %cb.1, f32[2,128]{1,0:T(2,128)} %gain.1, f32[2,128]{1,0:T(2,128)} %nb.1, bf16[2,128,512]{2,1,0:T(8,128)(2,1)} %W1.1, f32[2,512]{1,0:T(2,128)} %b1.1, ...), custom_call_target="tpu_custom_call" | custom-call | tf_op jit(solution)/shard_map/forecast/pallas_call | solution.py:369
  53.1 2.7 %copy.14 = bf16[48,128,128]{2,1,0:T(8,128)(2,1)} copy(bf16[48,128,128]{2,1,0:T(8,128)(2,1)} %forecast.1) | data formatting | bytes 3145728

commit v2 on v1

v2 whole, which is shorter than its diff:
```python
import functools

import jax
import jax.numpy as jnp
from jax import lax
from jax.experimental import pallas as pl
from jax.experimental.pallas import tpu as pltpu
from jax.sharding import PartitionSpec as P

BF, F = jnp.bfloat16, jnp.float32
R = 4
ROWS, COLS, C = 48, 128, 128
N = ROWS // R
MESH = pl.DeviceIdType.MESH
VMB = 60
TAIL = 8
HALF = 0.7071067811865476
SPAN = ((0, 12), (12, 26), (4, 10))


def iota(shape, d):
    return lax.broadcasted_iota(jnp.int32, shape, d)


def onehot(cond):
    return jnp.where(cond, 1.0, 0.0).astype(BF)


def dot(a, b):
    return jnp.dot(a, b, preferred_element_type=F)


def tree(v):
    while len(v) > 1:
        v = [v[i] + v[i + 1] if i + 1 < len(v) else v[i] for i in range(0, len(v), 2)]
    return v[0]


ORDER = ([1, 2, 3, 4, 5, 6, 7, 0, 11, 8, 9, 10], [2, 3, 4, 5, 6, 1, 7, 8, 9, 10, 0, 11])


def chunk(b, q):
    if isinstance(q, int):
        return ORDER[b][q]
    if b == 0:
        return jnp.where(q < 7, q + 1, jnp.where(q == 7, 0, jnp.where(q == 8, 11, q - 1)))
    return jnp.where(q < 5, q + 2, jnp.where(q == 5, 1, jnp.where(q < 10, q + 1, (q - 10) * 11)))


def gate(pieces, marks, lo, hi):
    if not marks:
        return jnp.concatenate(pieces, 0)
    n = len(pieces)
    return jnp.concatenate([p + marks[lo + i * (hi - lo) // n] for i, p in enumerate(pieces)], 0)


def conv(XG, KF, bias, acc_ref, row0):
    marks = []
    for rr in range(R):
        acc = [bias] * 8
        for r in range(7):
            xs = [XG[row0 + rr + r, k] for k in range(14)]
            ws = []
            for s in range(7):
                w = KF[7 * r + s]
                ws.append(jnp.concatenate([w, w], 0).astype(BF))
            for k in range(8):
                part = tree([ws[s] * xs[k + s] for s in range(7)])
                acc[k] = acc[k] + part.astype(F)
            marks.append(part * BF(0))
        for k in range(8):
            acc_ref[rr * 128 + k * 16 : rr * 128 + k * 16 + 16, :] = acc[k]
    return marks


def norm(acc_ref, out_ref, gain, nb):
    c = acc_ref[...]
    cen = c - jnp.sum(c, axis=-1, keepdims=True) * (1 / 128)
    var = jnp.sum(cen * cen, axis=-1, keepdims=True)
    out_ref[...] = (cen * lax.rsqrt(var + 128e-6) * gain + nb).astype(BF)


def expand_hidden(nrm_ref, hid_ref, W1E, marks):
    ones = onehot(iota((R * 128, 128), 1) < 3)
    x = gate([nrm_ref[16 * i : 16 * i + 16] for i in range(R * 8)], marks, *SPAN[1])
    u = dot(jnp.concatenate([x, ones], 1), W1E[...])
    hid_ref[...] = (u * lax.erf(u) + u).astype(BF)


def kernel(
    fields, mask_in, CK, cb_in, gain_in, nb_in, W1, b1_in, W2, b2_in, ls_in, out,
    mask, cb, gain, nb, b1, b2, ls,
    NAT, XG0, XG1, CKV, KF, W1V, W1E, W2V, G4, H4, INS,
    acc, nrm, hid, EL, ER, LH, RH, FB, load_sem, send_sem, recv_sem, out_sem,
):
    lat, lon = lax.axis_index("lat"), lax.axis_index("lon")
    nlat, nlon = lax.axis_size("lat"), lax.axis_size("lon")
    right, left = lax.rem(lon + 1, nlon), lax.rem(lon + nlon - 1, nlon)
    fold = nlon - 1 - lon
    is_top, is_low = lat == nlat - 1, lat == 0
    not_top, not_low = lat < nlat - 1, lat > 0

    loads = [pltpu.make_async_copy(fields.at[pl.ds(12 * q, 12)], NAT.at[pl.ds(12 * q, 12)], load_sem.at[q]) for q in range(4)]
    loads += [
        pltpu.make_async_copy(CK, CKV, load_sem.at[4]),
        pltpu.make_async_copy(W1, W1V, load_sem.at[5]),
        pltpu.make_async_copy(W2, W2V, load_sem.at[6]),
        pltpu.make_async_copy(cb_in, cb, load_sem.at[7]),
        pltpu.make_async_copy(gain_in, gain, load_sem.at[8]),
        pltpu.make_async_copy(nb_in, nb, load_sem.at[9]),
        pltpu.make_async_copy(b1_in, b1, load_sem.at[10]),
        pltpu.make_async_copy(b2_in, b2, load_sem.at[11]),
        pltpu.make_async_copy(ls_in, ls, load_sem.at[12]),
    ]
    mask_load = pltpu.make_async_copy(mask_in, mask, load_sem.at[13])
    mask_load.start()
    for cp in loads:
        cp.start()

    barrier = pltpu.get_barrier_semaphore()

    def greet(a, o):
        pl.semaphore_signal(barrier, inc=1, device_id={"lat": a, "lon": o}, device_id_type=MESH)

    greet(lat, left)
    greet(lat, right)

    @pl.when(not_low)
    def _():
        greet(lat - 1, lon)

    @pl.when(not_top)
    def _():
        greet(lat + 1, lon)

    @pl.when(is_top)
    def _():
        greet(lat, fold)

    def remote(src, dst, i, j, a, o):
        return pltpu.make_async_remote_copy(
            src_ref=src, dst_ref=dst, send_sem=send_sem.at[i], recv_sem=recv_sem.at[j],
            device_id={"lat": a, "lon": o}, device_id_type=MESH,
        )

    n, c = iota((256, 128), 0), iota((256, 128), 1)
    col = 8 * (n % 16) + n // 16 - 3
    h, hc = iota((128, 128), 0), iota((128, 128), 1)
    for rr in range(R):
        en = n % 16 - 4 * rr
        okn = (en >= 0) & (en < 3)
        lsrc, rsrc = jnp.where(okn, en, -1), jnp.where(okn, 125 + en, -1)
        G4[rr] = onehot(jnp.where(n < 224, col, jnp.where(n < 240, lsrc, rsrc)) == c)
    f, fc = iota((160, 128), 0), iota((160, 128), 1)
    kk, g16 = f // 16, f % 16
    gsrc = jnp.where(kk < 3, g16 - 1, g16 + 1)
    hsrc = jnp.where((gsrc >= 0) & (gsrc < 16), jnp.where(kk < 3, kk + 5, kk - 3) * 16 + gsrc, -1)
    for p in range(R // 2):
        e = g16 - 4 * jnp.where(kk < 8, 2 * p, 2 * p + 1)
        src = jnp.where(kk % 2 == 0, e * 16, (5 + e) * 16 + 15)
        H4[p] = onehot(jnp.where(kk < 6, hsrc, jnp.where((e >= 0) & (e < 3), src, -1)) == fc)
    m, mc = iota((96 * R, 32), 0), iota((96 * R, 32), 1)
    mr, mk, mg = m // 96, (m % 96) // 16, m % 16
    INS[...] = onehot(jnp.where(mk < 3, jnp.where(mg == 0, 4 * mr + mk, -1), jnp.where(mg == 15, 13 + 4 * mr + mk, -1)) == mc)
    mask_load.wait()

    def pairs(b, lo, hi, base):
        a, z = 16 * lo, 16 * (hi - lo)
        return (
            remote(ER.at[b, pl.ds(a, z)], LH.at[b, pl.ds(a, z)], base, base, lat, right),
            remote(EL.at[b, pl.ds(a, z)], RH.at[b, pl.ds(a, z)], base + 1, base + 1, lat, left),
        )

    quarters = [pairs(0, 3 * q, 3 * q + 3, 2 * q) for q in range(4)]
    cols_a = pairs(1, 1, 5, 8)
    cols_b = pairs(1, 5, 8, 10)
    cols_c = pairs(1, 0, 1, 12) + pairs(1, 11, 12, 14)
    cols_d = pairs(1, 8, 9, 16)
    cols_e = pairs(1, 9, 11, 18)
    cols = [cp for p in quarters for cp in p] + [*cols_a, *cols_b, *cols_c, *cols_d, *cols_e]

    def rows(XG, b):
        i = 20 + 3 * b
        north = remote(XG.at[pl.ds(48, 3)], XG.at[pl.ds(0, 3)], i, i, lat + 1, lon)
        across = remote(XG.at[pl.ds(48, 3)], FB.at[b], i + 1, i + 1, lat, fold)
        south = remote(XG.at[pl.ds(3, 3)], XG.at[pl.ds(51, 3)], i + 2, i + 2, lat - 1, lon)
        return north, across, south

    rows0, rows1 = rows(XG0, 0), rows(XG1, 1)

    def send_rows(copies):
        north, across, south = copies
        pl.when(not_top)(north.start)
        pl.when(is_top)(across.start)
        pl.when(not_low)(south.start)

    def wait_rows(XG, b, copies):
        north, across, south = copies
        pl.when(not_low)(north.wait_recv)

        @pl.when(is_low)
        def _():
            XG[0:3] = jnp.zeros((3, 14, 16, 128), BF)

        pl.when(not_top)(south.wait_recv)

        @pl.when(is_top)
        def _():
            across.wait_recv()
            flip = onehot(iota((224, 224), 0) + iota((224, 224), 1) == 223)
            for j in range(3):
                XG[51 + j] = dot(flip, FB[b, 2 - j].reshape(224, 128)).astype(BF).reshape(14, 16, 128)

    def insert(XG, b, ch):
        at = pl.ds(pl.multiple_of(16 * ch, 16), 16)
        o = dot(INS[...], jnp.concatenate([LH[b, at], RH[b, at]], 0)).astype(BF)
        for rr in range(R):
            row = R * ch + rr + 3
            XG[row, 0:3] = XG[row, 0:3] + o[rr * 96 : rr * 96 + 48].reshape(3, 16, 128)
            XG[row, 11:14] = XG[row, 11:14] + o[rr * 96 + 48 : rr * 96 + 96].reshape(3, 16, 128)

    def edges(b, ch, el, er):
        at = pl.ds(pl.multiple_of(16 * ch, 16), 16)
        EL[b, at] = el.astype(BF)
        ER[b, at] = er.astype(BF)

    def prep(ch, carry):
        el = er = None
        for rr in range(R):
            row = R * ch + rr
            mrow = jnp.broadcast_to(mask[pl.ds(row, 1), :].astype(F), (16, 128)).astype(BF)
            lhs = (G4[rr].reshape(16, 16, 128) * mrow[None]).reshape(256, 128)
            o = dot(lhs, NAT[row])
            XG0[row + 3] = o[:224].astype(BF).reshape(14, 16, 128)
            el = o[224:240] if el is None else el + o[224:240]
            er = o[240:256] if er is None else er + o[240:256]
        edges(0, ch, el, er)
        return carry

    def landed(copies):
        for cp in copies:
            cp.wait_recv()

    def insert_all(XG, b, lo, hi):
        def one(ch, carry):
            insert(XG, b, ch)
            return carry

        lax.fori_loop(lo, hi, one, 0)

    for i, q in enumerate((0, 3, 1, 2)):
        loads[q].wait()
        lax.fori_loop(3 * q, 3 * q + 3, prep, 0)
        if i == 0:
            @pl.when(not_low)
            def _():
                pl.semaphore_wait(barrier, 4)

            @pl.when(is_low)
            def _():
                pl.semaphore_wait(barrier, 3)

        for cp in quarters[q]:
            cp.start()
    for cp in loads[4:]:
        cp.wait()
    for b in range(2):
        for t in range(49):
            KF[b, t] = jnp.broadcast_to(CKV[t, b : b + 1, :], (8, 128))
        W1E[b, :128] = W1V[b]
        bb = b1[b : b + 1] * HALF
        hi = bb.astype(BF).astype(F)
        lo = (bb - hi).astype(BF).astype(F)
        z = iota((128, 512), 0)
        W1E[b, 128:] = jnp.where(z == 0, hi, jnp.where(z == 1, lo, jnp.where(z == 2, bb - hi - lo, 0.0))).astype(BF)
    landed(quarters[0] + quarters[3])
    insert_all(XG0, 0, 0, 3)
    insert_all(XG0, 0, 9, 12)
    send_rows(rows0)

    def conv_stage(b, q, par):
        return conv((XG0, XG1)[b], KF.at[b], jnp.broadcast_to(cb[b : b + 1], (16, 128)), acc.at[par], R * chunk(b, q))

    def norm_stage(b, q, par, marks):
        norm(acc.at[par], nrm.at[par], gain[b : b + 1] * (HALF * 128**0.5), nb[b : b + 1] * HALF)

    def hidden_stage(b, q, par, marks):
        expand_hidden(nrm.at[par], hid.at[par], W1E.at[b], marks)

    def out_stage(b, q, par, marks):
        XG = (XG0, XG1)[b]
        ch = chunk(b, q)
        first = gate([hid[par, 16 * i : 16 * i + 16, :128] for i in range(R * 8)], marks, *SPAN[0])
        y = dot(jnp.concatenate([first, hid[par, :, 128:]], 1), W2V[b])
        y = (y + b2[b : b + 1] * (1 / HALF)) * (ls[b : b + 1] * HALF)
        xs = []
        for rr in range(R):
            row = R * ch + rr
            res = XG[row + 3, 3:11].reshape(128, 128).astype(F)
            x = (res + y[rr * 128 : rr * 128 + 128]).astype(BF)
            xs.append(x)
            if b == 0:
                XG1[row + 3, 3:11] = x.reshape(8, 16, 128)
            else:
                NAT[row] = x
        if b == 0:
            el = er = None
            for p in range(R // 2):
                o = dot(H4[p], jnp.concatenate(xs[2 * p : 2 * p + 2], 1))
                for i in range(2):
                    row = R * ch + 2 * p + i + 3
                    v = o[:, 128 * i : 128 * i + 128]
                    XG1[row, 0:3] = v[:48].astype(BF).reshape(3, 16, 128)
                    XG1[row, 11:14] = v[48:96].astype(BF).reshape(3, 16, 128)
                    a, z = v[96 + 32 * i : 112 + 32 * i], v[112 + 32 * i : 128 + 32 * i]
                    el, er = (a, z) if el is None else (el + a, er + z)
            edges(1, ch, el, er)

    def finish(ch):
        return pltpu.make_async_copy(NAT.at[pl.ds(R * ch, R)], out.at[pl.ds(R * ch, R)], out_sem.at[ch])

    stages = (out_stage, hidden_stage, norm_stage)

    def step(b, q, par):
        marks = conv_stage(b, q + 3, (par + 3) % 2)
        for d, stage in enumerate(stages):
            stage(b, q + d, (par + d) % 2, marks)

    def mixed(s):
        i = s + 3
        marks = conv_stage(i // N, i % N, i % 2) if i < 2 * N else []
        for d, stage in enumerate(stages):
            i = s + d
            if 0 <= i < 2 * N:
                stage(i // N, i % N, i % 2, marks)

    mixed(-3)
    landed(quarters[1] + quarters[2])
    insert_all(XG0, 0, 3, 9)
    mixed(-2)
    mixed(-1)

    def body0(j, carry):
        @pl.when(j == 2)
        def _():
            wait_rows(XG0, 0, rows0)
            for cp in cols_a:
                cp.start()

        step(0, 2 * j, 0)
        step(0, 2 * j + 1, 1)
        return carry

    lax.fori_loop(0, 4, body0, 0)
    for cp in cols_b:
        cp.start()
    mixed(8)
    for cp in cols_c:
        cp.start()
    landed(cols_a)
    insert_all(XG1, 1, 1, 5)
    mixed(9)
    for cp in cols_d:
        cp.start()
    mixed(10)
    landed(cols_b)
    insert_all(XG1, 1, 5, 8)
    mixed(11)
    for cp in cols_e:
        cp.start()
    landed(cols_c)
    insert(XG1, 1, 0)
    insert(XG1, 1, 11)
    send_rows(rows1)

    def body1(j, carry):
        @pl.when(j == 1)
        def _():
            landed(cols_d)
            insert(XG1, 1, 8)

        @pl.when(j == 2)
        def _():
            landed(cols_e)
            insert_all(XG1, 1, 9, 11)

        @pl.when(j == 3)
        def _():
            wait_rows(XG1, 1, rows1)

        step(1, 2 * j, 0)
        step(1, 2 * j + 1, 1)
        finish(chunk(1, 2 * j)).start()
        finish(chunk(1, 2 * j + 1)).start()
        return carry

    lax.fori_loop(0, 4, body1, 0)
    for s in range(20, 24):
        mixed(s)
        finish(chunk(1, s - N)).start()
    for cp in cols:
        cp.wait_send()
    for north, across, south in (rows0, rows1):
        pl.when(not_top)(north.wait_send)
        pl.when(is_top)(across.wait_send)
        pl.when(not_low)(south.wait_send)
    for ch in range(N):
        finish(ch).wait()


def ungroup(x, mask, out, xv, ov, mv, sem_in, sem_out):
    def fetch(q):
        return pltpu.make_async_copy(x.at[pl.ds(q * TAIL, TAIL)], xv.at[pl.ds(q * TAIL, TAIL)], sem_in.at[q])

    def put(q):
        return pltpu.make_async_copy(ov.at[pl.ds(q * TAIL, TAIL)], out.at[pl.ds(q * TAIL, TAIL)], sem_out.at[q])

    steps = ROWS // TAIL
    mask_load = pltpu.make_async_copy(mask, mv, sem_in.at[steps])
    mask_load.start()
    for q in range(steps):
        fetch(q).start()
    h, hc = iota((128, 128), 0), iota((128, 128), 1)
    order = onehot((h % 8) * 16 + h // 8 == hc)
    mask_load.wait()
    wet = jnp.transpose(mv[...].astype(F))
    for q in range(steps):
        fetch(q).wait()
        for p in range(q * TAIL, q * TAIL + TAIL, 2):
            o = dot(order, jnp.concatenate([xv[p], xv[p + 1]], 1))
            for i in range(2):
                ov[p + i] = (o[:, 128 * i : 128 * i + 128] * wet[:, p + i : p + i + 1]).astype(BF)
        put(q).start()
    for q in range(steps):
        put(q).wait()


def shards(fields, wet_mask, *w):
    CK, cb, gain, nb, W1, b1, W2, b2, ls = w
    V = pltpu.VMEM
    grouped = pl.pallas_call(
        kernel,
        out_shape=jax.ShapeDtypeStruct((ROWS, COLS, C), BF),
        in_specs=[pl.BlockSpec(memory_space=pltpu.HBM)] * 11,
        out_specs=pl.BlockSpec(memory_space=pl.ANY),
        scratch_shapes=[
            V((ROWS, COLS), jnp.int32), V((2, C), F), V((2, C), F), V((2, C), F), V((2, 512), F), V((2, C), F), V((2, C), F),
            V((ROWS, COLS, C), BF), V((54, 14, 16, C), BF), V((54, 14, 16, C), BF),
            V((49, 2, C), F), V((2, 49, 8, C), F), V((2, 128, 512), BF), V((2, 256, 512), BF), V((2, 512, 128), BF),
            V((R, 256, 128), BF), V((R // 2, 160, 128), BF), V((96 * R, 32), BF),
            V((2, R * 128, C), F), V((2, R * 128, C), BF), V((2, R * 128, 512), BF),
            V((2, 192, C), BF), V((2, 192, C), BF), V((2, 192, C), BF), V((2, 192, C), BF), V((2, 3, 14, 16, C), BF),
            pltpu.SemaphoreType.DMA((14,)), pltpu.SemaphoreType.DMA((26,)), pltpu.SemaphoreType.DMA((26,)), pltpu.SemaphoreType.DMA((N,)),
        ],
        compiler_params=pltpu.CompilerParams(vmem_limit_bytes=VMB << 20, collective_id=0, has_side_effects=True),
        name="forecast",
    )(fields, wet_mask, jnp.transpose(CK, (1, 0, 2)), *w[1:])
    return pl.pallas_call(
        ungroup,
        out_shape=jax.ShapeDtypeStruct((ROWS, COLS, C), BF),
        in_specs=[pl.BlockSpec(memory_space=pl.ANY)] * 2,
        out_specs=pl.BlockSpec(memory_space=pl.ANY),
        scratch_shapes=[
            V((ROWS, COLS, C), BF), V((ROWS, COLS, C), BF), V((ROWS, COLS), jnp.int32),
            pltpu.SemaphoreType.DMA((ROWS // TAIL + 1,)), pltpu.SemaphoreType.DMA((ROWS // TAIL,)),
        ],
        compiler_params=pltpu.CompilerParams(vmem_limit_bytes=VMB << 20),
        name="ungroup",
    )(grouped, wet_mask)


def solution(mesh):
    return jax.shard_map(
        shards, mesh=mesh, in_specs=(P("lat", "lon", None), P("lat", "lon")) + (P(),) * 9,
        out_specs=P("lat", "lon", None), check_vma=False,
    )
```

time: 56.1 us -> 46.9 us (0.84)
  Pallas kernels: 51.7 us -> 46.6 us
  local copies, waits for them, and re-layouts: 4.16 us -> 0 us
    pallas_call x1, Pallas kernels: 51.7 us -> 43.3 us  [shards(): pl.pallas_call(kernel, out_shape=jax.ShapeDtypeStruct((ROWS, COLS, C), BF...]
    unnamed x2 -> x0, local copies, waits for them, and re-layouts: 4.16 us -> none
    pallas_call x0 -> x1, Pallas kernels: none -> 3.23 us  [shards(): pl.pallas_call(ungroup, out_shape=jax.ShapeDtypeStruct((ROWS, COLS, C), B...]
where the time goes in v2:
time: 46.9 us; the launch traced here: 46.7 us
  Pallas kernels  46.6 us (99%)
    pallas_call x1, Pallas kernels, shards(): pl.pallas_call(kernel, out_shape=jax.ShapeDtypeStruct((ROWS, COLS, C), BF...  43.3 us
    pallas_call x1, Pallas kernels, shards(): pl.pallas_call(ungroup, out_shape=jax.ShapeDtypeStruct((ROWS, COLS, C), B...  3.23 us

profile of v2, /device:TPU:4, one launch (start us, length us, event | category | flops | bytes accessed | tf_op | source)
XLA Modules:
  0.0 46.7 jit_solution(9797704811152545893)
XLA Ops:
  0.0 43.3 %forecast.1.x = bf16[48,128,128]{2,1,0:T(8,128)(2,1)} custom-call(bf16[48,128,128]{2,1,0:T(8,128)(2,1)} %fields.1, s32[48,128]{1,0:T(8,128)} %mask.1, f32[49,2,128]{2,1,0:T(2,128)} %bitcast.1, f32[2,128]{1,0:T(2,128)} %cb_in.1, f32[2,128]{1,0:T(2,128)} %gain_in.1, f32[2,128]{1,0:T(2,128)} %nb_in.1, bf16[2,128,512]{2,1,0:T(8,128)(2,1)} %W1.1, ...), custom_call_target="tpu_custom_call" | custom-call | tf_op jit(solution)/shard_map/forecast/pallas_call | solution.py:441
  43.4 3.2 %ungroup.1 = bf16[48,128,128]{2,1,0:T(8,128)(2,1)} custom-call(bf16[48,128,128]{2,1,0:T(8,128)(2,1)} %forecast.1.x, s32[48,128]{1,0:T(8,128)} %mask.1), custom_call_target="tpu_custom_call" | custom-call | tf_op jit(solution)/shard_map/ungroup/pallas_call | solution.py:458
